TPU v7x, 32 devices: a whole 2x2x4 slice. The times are simulated.
32 devices in a mesh: shard: 2 (over x), ctx: 4 (over y, core), tp: 4 (over z).
Axes of the slice: x: 2, y: 2, z: 4, core: 2. Of those that a mesh axis runs over, the one named last changes fastest.
Arguments:
- tokens: bfloat16 [4, 4096, 1024], P('shard', ('ctx', 'tp')), may hold values from -6 to 6
- positions: int32 [4, 4096], P('shard', 'ctx'), may hold values from 0 to 12287, as said below
- first_gain: float32 [1024], replicated, may hold values from 0.5 to 1.5
- query_weight: bfloat16 [1024, 1024], P(('shard', 'ctx'), 'tp'), may hold values from -0.1875 to 0.1875
- key_weight: bfloat16 [1024, 512], P(('shard', 'ctx'), 'tp'), may hold values from -0.1875 to 0.1875
- value_weight: bfloat16 [1024, 512], P(('shard', 'ctx'), 'tp'), may hold values from -0.1875 to 0.1875
- query_gain: float32 [64], replicated, may hold values from 0.1 to 1.9
- key_gain: float32 [64], replicated, may hold values from 0.1 to 1.9
- output_weight: bfloat16 [1024, 1024], P('tp', ('shard', 'ctx')), may hold values from -1 to 1
- second_gain: float32 [1024], replicated, may hold values from 0.5 to 1.5
- gate_weight: bfloat16 [1024, 4608], P(('shard', 'ctx'), 'tp'), may hold values from -0.1875 to 0.1875
- up_weight: bfloat16 [1024, 4608], P(('shard', 'ctx'), 'tp'), may hold values from -0.1875 to 0.1875
- down_weight: bfloat16 [4608, 1024], P('tp', ('shard', 'ctx')), may hold values from -0.09375 to 0.09375
- upstream: bfloat16 [4, 4096, 1024], P('shard', ('ctx', 'tp')), may hold values from -6 to 6
Outputs:
- block_output: bfloat16 [4, 4096, 1024], P('shard', ('ctx', 'tp'))
- token_gradient: float32 [4, 4096, 1024], P('shard', ('ctx', 'tp'))
- query_gradient: float32 [1024, 1024], P(('shard', 'ctx'), 'tp')
- key_gradient: float32 [1024, 512], P(('shard', 'ctx'), 'tp')
- value_gradient: float32 [1024, 512], P(('shard', 'ctx'), 'tp')
- output_gradient: float32 [1024, 1024], P('tp', ('shard', 'ctx'))
- gate_gradient: float32 [1024, 4608], P(('shard', 'ctx'), 'tp')
- up_gradient: float32 [1024, 4608], P(('shard', 'ctx'), 'tp')
- down_gradient: float32 [4608, 1024], P('tp', ('shard', 'ctx'))
- first_gain_gradient: float32 [1024], replicated
- second_gain_gradient: float32 [1024], replicated
- query_gain_gradient: float32 [64], replicated
- key_gain_gradient: float32 [64], replicated
Inputs may be any that keep to these rules, and one draw needn't show every extreme that they name: `positions`: along each sequence a position exceeds the one before it by 1 to 3; the first is at most 2.
All inputs are finite; a program needn't handle non-finite values.
Results may differ from a plain program's by a relative error of at most 0.02.
Values may be sent and summed in bfloat16 or wider, within the bound.
No kernel may reach another device: no remote copies, remote signals or barrier semaphores. Data moves between devices by JAX's collectives and lax.ppermute only.
A program may use at most 192 MiB of HBM per device.

v0:
```python
import math
import jax
import jax.numpy as jnp
from jax import lax
from jax.sharding import PartitionSpec as P

EPS = 1e-05
THETA = 1000000.0
NEGATIVE = -1e30


def norm_rows(values, gain):
    return values * lax.rsqrt(jnp.mean(values * values, axis=-1, keepdims=True) + EPS) * gain


def rotary_tables(places, width):
    freqs = jnp.exp(-math.log(THETA) * jnp.arange(0, width, 2).astype(jnp.float32) / width)
    angles = places.astype(jnp.float32)[:, None] * freqs[None, :]
    cosine = jnp.concatenate([jnp.cos(angles), jnp.cos(angles)], axis=-1)[:, None, :]
    sine = jnp.concatenate([jnp.sin(angles), jnp.sin(angles)], axis=-1)[:, None, :]
    return (cosine, sine)


def shape_heads(raw, gain, cosine, sine):
    normed = norm_rows(raw, gain)
    half = normed.shape[-1] // 2
    turned = jnp.concatenate([-normed[..., half:], normed[..., :half]], axis=-1)
    return normed * cosine + turned * sine


def dot_first(left, right):
    return lax.dot_general(
        left, right, (((0,), (0,)), ((), ())), preferred_element_type=jnp.float32
    )


def dot_last(left, right):
    return lax.dot_general(
        left, right, (((1,), (1,)), ((), ())), preferred_element_type=jnp.float32
    )


def project_rows(left, right):
    return jnp.dot(left, right, preferred_element_type=jnp.float32)


def project_pair(gate_back, gate_full, up_back, up_full):
    first_part = dot_last(gate_back, gate_full)
    return first_part + dot_last(up_back, up_full)


def project_three(query_back, query_full, key_back, key_full, value_back, value_full):
    total = dot_last(query_back, query_full)
    total = total + dot_last(key_back, key_full)
    return total + dot_last(value_back, value_full)


def fetch_weights(
    query_weight, key_weight, value_weight, output_weight, gate_weight, up_weight, down_weight
):
    return (
        lax.all_gather(query_weight, ("shard", "ctx"), axis=0, tiled=True),
        lax.all_gather(key_weight, ("shard", "ctx"), axis=0, tiled=True),
        lax.all_gather(value_weight, ("shard", "ctx"), axis=0, tiled=True),
        lax.all_gather(output_weight, ("shard", "ctx"), axis=1, tiled=True),
        lax.all_gather(gate_weight, ("shard", "ctx"), axis=0, tiled=True),
        lax.all_gather(up_weight, ("shard", "ctx"), axis=0, tiled=True),
        lax.all_gather(down_weight, ("shard", "ctx"), axis=1, tiled=True),
    )


def attend(query_b, key_b, value_b, first_query):
    span_rows, kv_heads, group, width = query_b.shape
    scale = 1.0 / math.sqrt(width)
    query_index = first_query + jnp.arange(span_rows)
    last_query = first_query + span_rows - 1
    init = (
        jnp.full((kv_heads, group, span_rows), NEGATIVE, jnp.float32),
        jnp.zeros((kv_heads, group, span_rows), jnp.float32),
        jnp.zeros((kv_heads, group, span_rows, width), jnp.float32),
    )
    key_piece = lax.all_gather(key_b, "ctx", axis=0, tiled=True)
    value_piece = lax.all_gather(value_b, "ctx", axis=0, tiled=True)

    def update(state):
        peak, total, accum = state
        scores = (
            jnp.einsum("qkgd,nkd->kgqn", query_b, key_piece, preferred_element_type=jnp.float32)
            * scale
        )
        key_index = jnp.arange(key_piece.shape[0])
        allowed = key_index[None, :] <= query_index[:, None]
        masked = jnp.where(allowed, scores, NEGATIVE)
        new_peak = jnp.maximum(peak, jnp.max(masked, axis=-1))
        weights = jnp.where(allowed, jnp.exp(masked - new_peak[..., None]), 0.0)
        total = jnp.sum(weights, axis=-1)
        accum = jnp.einsum(
            "kgqn,nkd->kgqd",
            weights.astype(jnp.bfloat16),
            value_piece,
            preferred_element_type=jnp.float32,
        )
        return (new_peak, total, accum)

    peak, total, accum = lax.cond(jnp.int32(0) <= last_query, update, lambda state: state, init)
    return (accum / total[..., None], peak + jnp.log(total))


def attend_back(query_b, keys_all, values_all, back_b, attention, logsum, first_query):
    span_rows, kv_heads, group, width = query_b.shape
    scale = 1.0 / math.sqrt(width)
    query_index = first_query + jnp.arange(span_rows)
    delta = jnp.einsum("qkgd,kgqd->kgq", back_b.astype(jnp.float32), attention)

    def block(index, carry):
        query_back, key_buffer, value_buffer = carry
        key_block = lax.dynamic_slice_in_dim(keys_all, index * span_rows, span_rows, 0)
        value_block = lax.dynamic_slice_in_dim(values_all, index * span_rows, span_rows, 0)
        scores = (
            jnp.einsum("qkgd,nkd->kgqn", query_b, key_block, preferred_element_type=jnp.float32)
            * scale
        )
        key_index = index * span_rows + jnp.arange(span_rows)
        allowed = key_index[None, :] <= query_index[:, None]
        probs = jnp.where(allowed, jnp.exp(scores - logsum[..., None]), 0.0)
        value_part = jnp.einsum(
            "kgqn,qkgd->nkd", probs.astype(jnp.bfloat16), back_b, preferred_element_type=jnp.float32
        )
        slopes = jnp.einsum(
            "qkgd,nkd->kgqn", back_b, value_block, preferred_element_type=jnp.float32
        )
        score_back = (probs * (slopes - delta[..., None])).astype(jnp.bfloat16)
        query_back = (
            query_back
            + jnp.einsum(
                "kgqn,nkd->qkgd", score_back, key_block, preferred_element_type=jnp.float32
            )
            * scale
        )
        key_part = (
            jnp.einsum("kgqn,qkgd->nkd", score_back, query_b, preferred_element_type=jnp.float32)
            * scale
        )
        key_buffer = lax.dynamic_update_slice_in_dim(key_buffer, key_part, index * span_rows, 0)
        value_buffer = lax.dynamic_update_slice_in_dim(
            value_buffer, value_part, index * span_rows, 0
        )
        return (query_back, key_buffer, value_buffer)

    init = (
        jnp.zeros(query_b.shape, jnp.float32),
        jnp.zeros(keys_all.shape, jnp.float32),
        jnp.zeros(values_all.shape, jnp.float32),
    )
    return lax.fori_loop(0, first_query // span_rows + 1, block, init)


def per_device(
    tokens,
    positions,
    first_gain,
    query_weight,
    key_weight,
    value_weight,
    query_gain,
    key_gain,
    output_weight,
    second_gain,
    gate_weight,
    up_weight,
    down_weight,
    upstream,
):
    sequences, rows, width = tokens.shape
    span_rows = positions.shape[1]
    head_dim = query_gain.shape[0]
    first_query = lax.axis_index("ctx") * span_rows
    query_acc = jnp.zeros((width, query_weight.shape[1]), jnp.float32)
    key_acc = jnp.zeros((width, key_weight.shape[1]), jnp.float32)
    value_acc = jnp.zeros((width, value_weight.shape[1]), jnp.float32)
    output_acc = jnp.zeros((output_weight.shape[0], width), jnp.float32)
    gate_acc = jnp.zeros((width, gate_weight.shape[1]), jnp.float32)
    up_acc = jnp.zeros((width, up_weight.shape[1]), jnp.float32)
    down_acc = jnp.zeros((down_weight.shape[0], width), jnp.float32)
    first_gain_acc = jnp.zeros_like(first_gain)
    second_gain_acc = jnp.zeros_like(second_gain)
    query_gain_acc = jnp.zeros_like(query_gain)
    key_gain_acc = jnp.zeros_like(key_gain)
    results = []
    gradients = []
    for seq in range(sequences):
        current = fetch_weights(
            query_weight,
            key_weight,
            value_weight,
            output_weight,
            gate_weight,
            up_weight,
            down_weight,
        )
        query_full, key_full, value_full, output_full, gate_full, up_full, down_full = current
        token_rows = tokens[seq].astype(jnp.float32)
        first = norm_rows(token_rows, first_gain).astype(jnp.bfloat16)
        first_all = lax.all_gather(first, "tp", axis=0, tiled=True)
        cosine, sine = rotary_tables(positions[seq], head_dim)
        query_raw = jnp.dot(first_all, query_full, preferred_element_type=jnp.float32).reshape(
            span_rows, -1, head_dim
        )
        key_raw = jnp.dot(first_all, key_full, preferred_element_type=jnp.float32).reshape(
            span_rows, -1, head_dim
        )
        value_b = (
            jnp.dot(first_all, value_full, preferred_element_type=jnp.float32)
            .astype(jnp.bfloat16)
            .reshape(span_rows, -1, head_dim)
        )
        kv_heads = key_raw.shape[1]
        group = query_raw.shape[1] // kv_heads

        def query_shape(raw, gain):
            return shape_heads(raw, gain, cosine, sine)

        query_b = (
            query_shape(query_raw, query_gain)
            .astype(jnp.bfloat16)
            .reshape(span_rows, kv_heads, group, head_dim)
        )
        key_b = query_shape(key_raw, key_gain).astype(jnp.bfloat16)
        attention, logsum = attend(query_b, key_b, value_b, first_query)
        mixed_b = jnp.transpose(attention, (2, 0, 1, 3)).reshape(span_rows, -1).astype(jnp.bfloat16)
        attn_rows = lax.psum_scatter(
            project_rows(mixed_b, output_full).astype(jnp.bfloat16),
            "tp",
            scatter_dimension=0,
            tiled=True,
        ).astype(jnp.float32)
        middle = token_rows + attn_rows
        second = norm_rows(middle, second_gain).astype(jnp.bfloat16)
        second_all = lax.all_gather(second, "tp", axis=0, tiled=True)
        gate = jnp.dot(second_all, gate_full, preferred_element_type=jnp.float32)
        up = jnp.dot(second_all, up_full, preferred_element_type=jnp.float32)
        gate_sig = jax.nn.sigmoid(gate)
        swish = gate * gate_sig
        hidden_b = (swish * up).astype(jnp.bfloat16)
        ffn_rows = lax.psum_scatter(
            project_rows(hidden_b, down_full).astype(jnp.bfloat16),
            "tp",
            scatter_dimension=0,
            tiled=True,
        ).astype(jnp.float32)
        results.append((middle + ffn_rows).astype(jnp.bfloat16))
        current = fetch_weights(
            query_weight,
            key_weight,
            value_weight,
            output_weight,
            gate_weight,
            up_weight,
            down_weight,
        )
        query_full, key_full, value_full, output_full, gate_full, up_full, down_full = current
        upstream_b = upstream[seq]
        upstream_all = lax.all_gather(upstream_b, "tp", axis=0, tiled=True)
        down_acc = down_acc + dot_first(hidden_b, upstream_all)
        hidden_back = dot_last(upstream_all, down_full)
        gate_back = (hidden_back * up * (gate_sig * (1.0 + gate * (1.0 - gate_sig)))).astype(
            jnp.bfloat16
        )
        up_back = (hidden_back * swish).astype(jnp.bfloat16)
        gate_acc = gate_acc + dot_first(second_all, gate_back)
        up_acc = up_acc + dot_first(second_all, up_back)
        second_back = lax.psum_scatter(
            project_pair(gate_back, gate_full, up_back, up_full).astype(jnp.bfloat16),
            "tp",
            scatter_dimension=0,
            tiled=True,
        ).astype(jnp.float32)
        unused_second, second_fn = jax.vjp(norm_rows, middle, second_gain)
        middle_part, second_part = second_fn(second_back)
        second_gain_acc = second_gain_acc + second_part
        middle_back = upstream_b.astype(jnp.float32) + middle_part
        mixed_back_all = lax.all_gather(middle_back.astype(jnp.bfloat16), "tp", axis=0, tiled=True)
        output_acc = output_acc + dot_first(mixed_b, mixed_back_all)
        attention_back = (
            dot_last(mixed_back_all, output_full)
            .astype(jnp.bfloat16)
            .reshape(span_rows, kv_heads, group, head_dim)
        )
        keys_all, values_all = (
            lax.all_gather(key_b, "ctx", axis=0, tiled=True),
            lax.all_gather(value_b, "ctx", axis=0, tiled=True),
        )
        query_back, key_buffer, value_buffer = attend_back(
            query_b, keys_all, values_all, attention_back, attention, logsum, first_query
        )
        key_back, value_back = (
            lax.psum_scatter(
                key_buffer.astype(jnp.bfloat16), "ctx", scatter_dimension=0, tiled=True
            ).astype(jnp.float32),
            lax.psum_scatter(
                value_buffer.astype(jnp.bfloat16), "ctx", scatter_dimension=0, tiled=True
            ).astype(jnp.float32),
        )
        value_back_b = value_back.reshape(span_rows, -1).astype(jnp.bfloat16)
        unused_key, key_fn = jax.vjp(query_shape, key_raw, key_gain)
        key_raw_back, key_gain_part = key_fn(key_back)
        unused_query, query_fn = jax.vjp(query_shape, query_raw, query_gain)
        query_raw_back, query_gain_part = query_fn(query_back.reshape(span_rows, -1, head_dim))
        key_raw_b = key_raw_back.reshape(span_rows, -1).astype(jnp.bfloat16)
        query_raw_b = query_raw_back.reshape(span_rows, -1).astype(jnp.bfloat16)
        key_gain_acc = key_gain_acc + key_gain_part
        query_gain_acc = query_gain_acc + query_gain_part
        query_acc = query_acc + dot_first(first_all, query_raw_b)
        key_acc = key_acc + dot_first(first_all, key_raw_b)
        value_acc = value_acc + dot_first(first_all, value_back_b)
        first_back = lax.psum_scatter(
            project_three(
                query_raw_b, query_full, key_raw_b, key_full, value_back_b, value_full
            ).astype(jnp.bfloat16),
            "tp",
            scatter_dimension=0,
            tiled=True,
        ).astype(jnp.float32)
        unused_first, first_fn = jax.vjp(norm_rows, token_rows, first_gain)
        token_part, first_part = first_fn(first_back)
        first_gain_acc = first_gain_acc + first_part
        gradients.append(middle_back + token_part)
    query_out, key_out, value_out, output_out, gate_out, up_out, down_out = (
        lax.psum_scatter(query_acc, ("shard", "ctx"), scatter_dimension=0, tiled=True),
        lax.psum_scatter(key_acc, ("shard", "ctx"), scatter_dimension=0, tiled=True),
        lax.psum_scatter(value_acc, ("shard", "ctx"), scatter_dimension=0, tiled=True),
        lax.psum_scatter(output_acc, ("shard", "ctx"), scatter_dimension=1, tiled=True),
        lax.psum_scatter(gate_acc, ("shard", "ctx"), scatter_dimension=0, tiled=True),
        lax.psum_scatter(up_acc, ("shard", "ctx"), scatter_dimension=0, tiled=True),
        lax.psum_scatter(down_acc, ("shard", "ctx"), scatter_dimension=1, tiled=True),
    )
    first_total, second_total, query_total, key_total = lax.psum(
        (first_gain_acc, second_gain_acc, query_gain_acc, key_gain_acc), ("shard", "ctx", "tp")
    )
    return (
        jnp.stack(results),
        jnp.stack(gradients),
        query_out,
        key_out,
        value_out,
        output_out,
        gate_out,
        up_out,
        down_out,
        first_total,
        second_total,
        query_total,
        key_total,
    )


def solution(mesh):
    in_specs = (
        P("shard", ("ctx", "tp"), None),
        P("shard", "ctx"),
        P(),
        P(("shard", "ctx"), "tp"),
        P(("shard", "ctx"), "tp"),
        P(("shard", "ctx"), "tp"),
        P(),
        P(),
        P("tp", ("shard", "ctx")),
        P(),
        P(("shard", "ctx"), "tp"),
        P(("shard", "ctx"), "tp"),
        P("tp", ("shard", "ctx")),
        P("shard", ("ctx", "tp"), None),
    )
    out_specs = (
        P("shard", ("ctx", "tp"), None),
        P("shard", ("ctx", "tp"), None),
        P(("shard", "ctx"), "tp"),
        P(("shard", "ctx"), "tp"),
        P(("shard", "ctx"), "tp"),
        P("tp", ("shard", "ctx")),
        P(("shard", "ctx"), "tp"),
        P(("shard", "ctx"), "tp"),
        P("tp", ("shard", "ctx")),
        P(),
        P(),
        P(),
        P(),
    )
    return jax.shard_map(
        per_device, mesh=mesh, in_specs=in_specs, out_specs=out_specs, check_vma=False
    )
```

profile of v0, /device:TPU:0, one launch (start us, length us, event | category | flops | bytes accessed | tf_op | source)
XLA Modules:
  0.0 1653.8 jit_solution(1743868269783206539)
XLA Ops:
  26.7 35.4 %all-gather.18.cloned.1.call-done = bf16[1024,1024]{1,0:T(8,128)(2,1)} async-done(((bf16[256,1024]{1,0:T(8,128)(2,1)}), bf16[1024,1024]{1,0:T(8,128)(2,1)}) %all-gather.18.cloned.1.call-update) | async-done | bytes 2097168 | tf_op jit(solution)/shard_map/all_gather | solution.py:204
  65.1 43.7 %all-gather.32.cloned.1.call-done = bf16[1024,1024]{1,0:T(8,128)(2,1)} async-done(((bf16[256,1024]{1,0:T(8,128)(2,1)}), bf16[1024,1024]{1,0:T(8,128)(2,1)}) %all-gather.32.cloned.1.call-update) | async-done | bytes 2097168 | tf_op jit(solution)/shard_map/all_gather | solution.py:204
  164.3 84.7 %conditional.2 = (f32[2,2,1024]{2,1,0:T(2,128)}, f32[2,2,1024]{2,1,0:T(2,128)}, f32[2,2,1024,64]{2,3,1,0:T(8,128)S(1)}, f32[2,2,1024]{2,1,0:T(2,128)S(1)}) conditional(s32[]{:T(128)} %convert_element_type.260, () %tuple.36, (s32[1024]{0:T(1024)S(1)}, bf16[4096,2,64]{0,2,1:T(8,128)(2,1)}, bf16[1024,2,2,64]{0,3,2,1:T(8,128)(2,1)}, ...), branch_computations={%region_3.0_spmd, %region_4.7_spmd} | conditional | flops 4517261312 | bytes 226103360 | solution.py:105
  252.9 83.4 %conditional.3 = (f32[2,2,1024]{2,1,0:T(2,128)}, f32[2,2,1024]{2,1,0:T(2,128)}, f32[2,2,1024,64]{2,3,1,0:T(8,128)S(1)}, f32[2,2,1024]{2,1,0:T(2,128)S(1)}) conditional(s32[]{:T(128)} %convert_element_type.260, () %tuple.38, (s32[1024]{0:T(1024)S(1)}, bf16[4096,2,64]{0,2,1:T(8,128)(2,1)}, bf16[1024,2,2,64]{0,3,2,1:T(8,128)(2,1)S(1)}, ...), branch_computations={%region_13.14_spmd, %region_14.17_spmd} | conditional | flops 4517261312 | bytes 230297696 | solution.py:105
  340.0 42.3 %reduce-scatter.24.cloned.1.call-done = bf16[256,1024]{1,0:T(8,128)(2,1)} async-done(((bf16[1024,1024]{1,0:T(8,128)(2,1)}), bf16[256,1024]{1,0:T(8,128)(2,1)}) %reduce-scatter.24.cloned.1.call-update) | async-done | bytes 524304 | tf_op jit(solution)/shard_map/reduce_scatter | solution.py:231
  391.0 40.7 %all-gather.24.cloned.1.call-done = bf16[1024,1024]{1,0:T(8,128)(2,1)} async-done(((bf16[256,1024]{1,0:T(8,128)(2,1)}), bf16[1024,1024]{1,0:T(8,128)(2,1)}) %all-gather.24.cloned.1.call-update) | async-done | bytes 2097168 | tf_op jit(solution)/shard_map/all_gather | solution.py:239
  468.6 40.3 %all-gather.44.cloned.1.call-done = bf16[1,1024,1024]{2,1,0:T(8,128)(2,1)} async-done(((bf16[1,256,1024]{2,1,0:T(8,128)(2,1)}), bf16[1,1024,1024]{2,1,0:T(8,128)(2,1)}) %all-gather.44.cloned.1.call-update) | async-done | bytes 2097168 | tf_op jit(solution)/shard_map/all_gather | solution.py:263
  557.4 49.3 %all-gather.38.cloned.1.call-done = bf16[1024,1024]{1,0:T(8,128)(2,1)} async-done(((bf16[256,1024]{1,0:T(8,128)(2,1)}), bf16[1024,1024]{1,0:T(8,128)(2,1)}) %all-gather.38.cloned.1.call-update) | async-done | bytes 2097168 | tf_op jit(solution)/shard_map/all_gather | solution.py:239
  618.6 36.3 %all-gather.46.cloned.1.call-done = bf16[1,1024,1024]{2,1,0:T(8,128)(2,1)} async-done(((bf16[1,256,1024]{2,1,0:T(8,128)(2,1)}), bf16[1,1024,1024]{2,1,0:T(8,128)(2,1)}) %all-gather.46.cloned.1.call-update) | async-done | bytes 2097168 | tf_op jit(solution)/shard_map/all_gather | solution.py:263
  680.7 35.6 %reduce-scatter.36.cloned.1.call-done = bf16[256,1024]{1,0:T(8,128)(2,1)} async-done(((bf16[1024,1024]{1,0:T(8,128)(2,1)}), bf16[256,1024]{1,0:T(8,128)(2,1)}) %reduce-scatter.36.cloned.1.call-update) | async-done | bytes 524304 | tf_op jit(solution)/shard_map/reduce_scatter | solution.py:272
  719.1 42.7 %reduce-scatter.26.cloned.1.call-done = bf16[256,1024]{1,0:T(8,128)(2,1)} async-done(((bf16[1024,1024]{1,0:T(8,128)(2,1)}), bf16[256,1024]{1,0:T(8,128)(2,1)}) %reduce-scatter.26.cloned.1.call-update) | async-done | bytes 524304 | tf_op jit(solution)/shard_map/reduce_scatter | solution.py:245
  767.1 43.3 %all-gather.40.cloned.1.call-done = bf16[1024,1024]{1,0:T(8,128)(2,1)} async-done(((bf16[256,1024]{1,0:T(8,128)(2,1)}), bf16[1024,1024]{1,0:T(8,128)(2,1)}) %all-gather.40.cloned.1.call-update) | async-done | bytes 2097168 | tf_op jit(solution)/shard_map/all_gather | solution.py:282
  815.4 35.1 %while.30 = (s32[]{:T(128)}, f32[1024,2,2,64]{0,3,2,1:T(8,128)S(1)}, bf16[4096,2,64]{0,2,1:T(8,128)(2,1)}, bf16[4096,2,64]{0,2,1:T(8,128)(2,1)}, s32[]{:T(128)},...) while((s32[]{:T(128)}, ...), condition=%wide.region_23.24_spmd.clone, body=%wide.region_22.23_spmd.clone.sunk | while | flops 2728003584 | bytes 93126936 | solution.py:155
  862.6 34.7 %while.31 = (s32[]{:T(128)}, f32[1024,2,2,64]{0,3,2,1:T(8,128)S(1)}, bf16[4096,2,64]{0,2,1:T(8,128)(2,1)}, bf16[4096,2,64]{0,2,1:T(8,128)(2,1)}, s32[]{:T(128)},...) while((s32[]{:T(128)}, ...), condition=%wide.region_33.34_spmd.clone, body=%wide.region_32.33_spmd.clone.sunk | while | flops 2728003584 | bytes 99418456 | solution.py:155
  910.4 68.9 %reduce-scatter.30.cloned.1.call-done = bf16[1024,2,64]{0,2,1:T(8,128)(2,1)} async-done(((bf16[4096,2,64]{0,2,1:T(8,128)(2,1)}), bf16[1024,2,64]{0,2,1:T(8,128)(2,1)}) %reduce-scatter.30.cloned.1.call-update) | async-done | bytes 262160 | tf_op jit(solution)/shard_map/reduce_scatter | solution.py:297
  980.5 142.9 %reduce-scatter.38.cloned.1.call-done = bf16[1024,2,64]{0,2,1:T(8,128)(2,1)} async-done(((bf16[4096,2,64]{0,2,1:T(8,128)(2,1)}), bf16[1024,2,64]{0,2,1:T(8,128)(2,1)}) %reduce-scatter.38.cloned.1.call-update) | async-done | bytes 262160 | tf_op jit(solution)/shard_map/reduce_scatter | solution.py:297
  1273.0 43.3 %reduce-scatter.22.cloned.1.call-done = bf16[256,1024]{1,0:T(8,128)(2,1)} async-done(((bf16[1024,1024]{1,0:T(8,128)(2,1)}), bf16[256,1024]{1,0:T(8,128)(2,1)}) %reduce-scatter.22.cloned.1.call-update) | async-done | bytes 524304 | tf_op jit(solution)/shard_map/reduce_scatter | solution.py:245
  1319.6 39.9 %all-reduce.8 = (f32[1024]{0:T(1024)}, f32[1024]{0:T(1024)}, f32[64]{0:T(128)}, f32[64]{0:T(128)}) all-reduce(f32[1024]{0:T(1024)S(1)} %add.369, f32[1024]{0:T(1024)S(1)} %add.370, f32[64]{0:T(128)S(1)} %add.371, f32[64]{0:T(128)S(1)} %add.372), channel_id=1, replica_groups=mesh['shard'=2,'ctx'=4,'tp'=4] {'shard','ctx','tp'}, use_global_device_ids=true, to_apply=%region_49.50 | all-reduce | flops 2176 | bytes 17408 | tf_op jit(solution)/shard_map/psum | solution.py:337
  1374.2 58.2 %reduce-scatter.54.cloned.1.call-done = f32[128,1152]{1,0:T(8,128)} async-done(((f32[1024,1152]{1,0:T(8,128)}), f32[128,1152]{1,0:T(8,128)}) %reduce-scatter.54.cloned.1.call-update) | async-done | bytes 589840 | tf_op jit(solution)/shard_map/reduce_scatter | solution.py:334
  1432.3 57.9 %reduce-scatter.56.cloned.1.call-done = f32[1152,128]{1,0:T(8,128)} async-done(((f32[1152,1024]{1,0:T(8,128)}), f32[1152,128]{1,0:T(8,128)}) %reduce-scatter.56.cloned.1.call-update) | async-done | bytes 589840 | tf_op jit(solution)/shard_map/reduce_scatter | solution.py:335
  1490.3 40.1 %reduce-scatter.44.cloned.1.call-done = f32[128,256]{1,0:T(8,128)} async-done(((f32[1024,256]{1,0:T(8,128)}), f32[128,256]{1,0:T(8,128)}) %reduce-scatter.44.cloned.1.call-update) | async-done | bytes 131088 | tf_op jit(solution)/shard_map/reduce_scatter | solution.py:329
  1530.4 40.1 %reduce-scatter.50.cloned.1.call-done = f32[256,128]{1,0:T(8,128)} async-done(((f32[256,1024]{1,0:T(8,128)}), f32[256,128]{1,0:T(8,128)}) %reduce-scatter.50.cloned.1.call-update) | async-done | bytes 131088 | tf_op jit(solution)/shard_map/reduce_scatter | solution.py:332
  1570.5 37.9 %reduce-scatter.46.cloned.1.call-done = f32[128,128]{1,0:T(8,128)} async-done(((f32[1024,128]{1,0:T(8,128)}), f32[128,128]{1,0:T(8,128)}) %reduce-scatter.46.cloned.1.call-update) | async-done | bytes 65552 | tf_op jit(solution)/shard_map/reduce_scatter | solution.py:330
  1608.5 37.7 %reduce-scatter.48.cloned.1.call-done = f32[128,128]{1,0:T(8,128)} async-done(((f32[1024,128]{1,0:T(8,128)}), f32[128,128]{1,0:T(8,128)}) %reduce-scatter.48.cloned.1.call-update) | async-done | bytes 65552 | tf_op jit(solution)/shard_map/reduce_scatter | solution.py:331
  (501 shorter events, 658.9 us)
Async XLA Ops:
  14.0 150.3 %all-gather.20.cloned.1.call-start = ((), (), s32[]{:S(2)}) async-start(), calls=%async_computation.20 | async-start | bytes 1310720 | tf_op jit(solution)/shard_map/all_gather | solution.py:82
  125.2 127.7 %all-gather.34.cloned.1.call-start = ((), (), s32[]{:S(2)}) async-start(), calls=%async_computation.29 | async-start | bytes 1310720 | tf_op jit(solution)/shard_map/all_gather | solution.py:82
  156.7 183.3 %reduce-scatter.20.cloned.1.call-start = ((), (), s32[]{:S(2)}) async-start(), calls=%async_computation.22 | async-start | bytes 2621440 | tf_op jit(solution)/shard_map/reduce_scatter | solution.py:231
  252.6 129.7 %reduce-scatter.24.cloned.1.call-start = ((), (), s32[]{:S(2)}) async-start(), calls=%async_computation.31 | async-start | bytes 2621440 | tf_op jit(solution)/shard_map/reduce_scatter | solution.py:231
  387.3 121.6 %all-gather.44.cloned.1.call-start = ((), (), s32[]{:S(2)}) async-start(), calls=%async_computation.51 | async-start | bytes 2621440 | tf_op jit(solution)/shard_map/all_gather | solution.py:263
  388.4 150.4 %all-gather.30.cloned.1.call-start = ((), (), s32[]{:S(2)}) async-start(), calls=%async_computation.26 | async-start | bytes 2654208 | tf_op jit(solution)/shard_map/all_gather | solution.py:68
  389.2 217.5 %all-gather.38.cloned.1.call-start = ((), (), s32[]{:S(2)}) async-start(), calls=%async_computation.32 | async-start | bytes 2621440 | tf_op jit(solution)/shard_map/all_gather | solution.py:239
  389.9 265.0 %all-gather.46.cloned.1.call-start = ((), (), s32[]{:S(2)}) async-start(), calls=%async_computation.52 | async-start | bytes 2621440 | tf_op jit(solution)/shard_map/all_gather | solution.py:263
  390.5 290.2 %reduce-scatter.28.cloned.1.call-start = ((), (), s32[]{:S(2)}) async-start(), calls=%async_computation.34 | async-start | bytes 2621440 | tf_op jit(solution)/shard_map/reduce_scatter | solution.py:272
  557.1 159.1 %reduce-scatter.36.cloned.1.call-start = ((), (), s32[]{:S(2)}) async-start(), calls=%async_computation.39 | async-start | bytes 2621440 | tf_op jit(solution)/shard_map/reduce_scatter | solution.py:272
  680.2 130.2 %all-gather.40.cloned.1.call-start = ((), (), s32[]{:S(2)}) async-start(), calls=%async_computation.35 | async-start | bytes 2621440 | tf_op jit(solution)/shard_map/all_gather | solution.py:282
  767.0 212.3 %reduce-scatter.30.cloned.1.call-start = ((), (), s32[]{:S(2)}) async-start(), calls=%async_computation.36 | async-start | bytes 1310720 | tf_op jit(solution)/shard_map/reduce_scatter | solution.py:297
  850.6 272.8 %reduce-scatter.38.cloned.1.call-start = ((), (), s32[]{:S(2)}) async-start(), calls=%async_computation.41 | async-start | bytes 1310720 | tf_op jit(solution)/shard_map/reduce_scatter | solution.py:297
  897.3 254.2 %reduce-scatter.32.cloned.1.call-start = ((), (), s32[]{:S(2)}) async-start(), calls=%async_computation.37 | async-start | bytes 1310720 | tf_op jit(solution)/shard_map/reduce_scatter | solution.py:300
  900.8 278.0 %reduce-scatter.40.cloned.1.call-start = ((), (), s32[]{:S(2)}) async-start(), calls=%async_computation.42 | async-start | bytes 1310720 | tf_op jit(solution)/shard_map/reduce_scatter | solution.py:300
  910.4 328.5 %reduce-scatter.34.cloned.1.call-start = ((), (), s32[]{:S(2)}) async-start(), calls=%async_computation.38 | async-start | bytes 2621440 | tf_op jit(solution)/shard_map/reduce_scatter | solution.py:316
  1184.4 131.9 %reduce-scatter.22.cloned.1.call-start = ((), (), s32[]{:S(2)}) async-start(), calls=%async_computation.27 | async-start | bytes 2621440 | tf_op jit(solution)/shard_map/reduce_scatter | solution.py:245
  1191.2 183.0 %reduce-scatter.52.cloned.1.call-start = ((), (), s32[]{:S(2)}) async-start(), calls=%async_computation.48 | async-start | bytes 5308416 | tf_op jit(solution)/shard_map/reduce_scatter | solution.py:333
  1201.3 231.0 %reduce-scatter.54.cloned.1.call-start = ((), (), s32[]{:S(2)}) async-start(), calls=%async_computation.49 | async-start | bytes 5308416 | tf_op jit(solution)/shard_map/reduce_scatter | solution.py:334
  1211.0 279.3 %reduce-scatter.56.cloned.1.call-start = ((), (), s32[]{:S(2)}) async-start(), calls=%async_computation.50 | async-start | bytes 5308416 | tf_op jit(solution)/shard_map/reduce_scatter | solution.py:335
  1221.4 309.0 %reduce-scatter.44.cloned.1.call-start = ((), (), s32[]{:S(2)}) async-start(), calls=%async_computation.44 | async-start | bytes 1179648 | tf_op jit(solution)/shard_map/reduce_scatter | solution.py:329
  1227.6 342.9 %reduce-scatter.50.cloned.1.call-start = ((), (), s32[]{:S(2)}) async-start(), calls=%async_computation.47 | async-start | bytes 1179648 | tf_op jit(solution)/shard_map/reduce_scatter | solution.py:332
  1231.9 376.6 %reduce-scatter.46.cloned.1.call-start = ((), (), s32[]{:S(2)}) async-start(), calls=%async_computation.45 | async-start | bytes 589824 | tf_op jit(solution)/shard_map/reduce_scatter | solution.py:330
  1235.5 410.7 %reduce-scatter.48.cloned.1.call-start = ((), (), s32[]{:S(2)}) async-start(), calls=%async_computation.46 | async-start | bytes 589824 | tf_op jit(solution)/shard_map/reduce_scatter | solution.py:331
  (147 other events, 6720.0 us)
Sparse Core Ops, SparseCore 0:
  13.4 48.6 all-gather.17
  64.2 44.5 all-gather.31
  131.7 17.8 all-gather.21
  151.0 17.9 all-gather.33
  170.4 16.7 all-gather.35
  252.7 42.6 reduce-scatter.19
  339.5 42.7 reduce-scatter.23
  557.2 63.3 reduce-scatter.27
  673.6 42.6 reduce-scatter.35
  718.6 43.1 reduce-scatter.25
  850.7 128.6 reduce-scatter.29
  981.9 141.4 reduce-scatter.37
  1126.5 24.8 reduce-scatter.31
  1153.8 24.8 reduce-scatter.39
  1181.6 43.8 reduce-scatter.33
  1227.6 43.1 reduce-scatter.41
  1273.1 43.1 reduce-scatter.21
  1320.3 53.8 reduce-scatter.51
  1378.4 53.8 reduce-scatter.53
  1436.4 53.8 reduce-scatter.55
  1494.3 36.0 reduce-scatter.43
  1534.5 35.9 reduce-scatter.49
  1574.3 34.0 reduce-scatter.45
  1612.1 34.0 reduce-scatter.47
  (1 shorter events, 15.5 us)
Sparse Core Ops, SparseCore 1:
  341.7 27.7 all-gather.25
  386.8 44.9 all-gather.23
  433.5 27.6 all-gather.27
  463.3 45.5 all-gather.43
  510.8 28.0 all-gather.29
  541.1 65.5 all-gather.37
  608.1 46.7 all-gather.45
  765.5 44.8 all-gather.39
  812.4 44.3 all-gather.41
where the time goes:
time: 1660 us; the launch traced here: 1650 us
  waiting for transfers between devices  1080 us (65%)
  matrix products  331 us (20%)
  other arithmetic  120 us (7%)
  blocking collectives  83.1 us (5%)
  local copies, waits for them, and re-layouts  20 us (1%)
  between operations  17.8 us (1%)
    reduce_scatter x2, waiting for transfers between devices, per_device(): lax.psum_scatter(key_buffer.astype(jnp.bfloat16), 'ctx', scatter_dimensio...  212 us
    all_gather x2, waiting for transfers between devices, per_device(): second_all = lax.all_gather(second, 'tp', axis=0, tiled=True)  90 us
    reduce_scatter x2, waiting for transfers between devices, per_device(): lax.psum_scatter(project_rows(hidden_b, down_full).astype(jnp.bfloat16),...  86 us
    all_gather x2, waiting for transfers between devices, per_device(): first_all = lax.all_gather(first, 'tp', axis=0, tiled=True)  79.1 us
    all_gather x2, waiting for transfers between devices, per_device(): upstream_all = lax.all_gather(upstream_b, 'tp', axis=0, tiled=True)  76.7 us
    dot_general x14, matrix products, dot_last(): lax.dot_general(left, right, (((1,), (1,)), ((), ())), preferred_element_...  64.4 us
    reduce_scatter x1, waiting for transfers between devices, per_device(): lax.psum_scatter(up_acc, ('shard', 'ctx'), scatter_dimension=0, tiled=True)  58.2 us
    reduce_scatter x1, waiting for transfers between devices, per_device(): lax.psum_scatter(down_acc, ('shard', 'ctx'), scatter_dimension=1, tiled=T...  57.9 us
  transfers between devices with their start and end apart: 34, of which 26 were waited for; matrix products, arithmetic and copies ran while one was open for 27% of the time, Pallas kernels for 0%

commit v1 on v0

--- a/solution.py
+++ b/solution.py
@@ -236,7 +236,14 @@
         ).astype(jnp.float32)
         middle = token_rows + attn_rows
         second = norm_rows(middle, second_gain).astype(jnp.bfloat16)
-        second_all = lax.all_gather(second, "tp", axis=0, tiled=True)
+        ring = [second]
+        for hop in range(3):
+            ring.append(lax.ppermute(ring[-1], "tp", [(dev, (dev + 1) % 4) for dev in range(4)]))
+        second_all = jnp.roll(
+            jnp.concatenate(ring[::-1], axis=0),
+            (lax.axis_index("tp") + 1) * ring[0].shape[0],
+            axis=0,
+        )
         gate = jnp.dot(second_all, gate_full, preferred_element_type=jnp.float32)
         up = jnp.dot(second_all, up_full, preferred_element_type=jnp.float32)
         gate_sig = jax.nn.sigmoid(gate)

time: 1660 us -> 1630 us (0.982)
  waiting for transfers between devices: 1080 us -> 1030 us
    all_gather x2 -> x0, waiting for transfers between devices: 90 us -> none  [per_device(): second_all = lax.all_gather(second, 'tp', axis=0, tiled=True)]
    ppermute x0 -> x6, waiting for transfers between devices: none -> 56 us  [per_device(): lax.ppermute(ring[-1], 'tp', [(dev, (dev + 1) % 4) for dev in range(4)])]
    reduce_scatter x1, waiting for transfers between devices: 58.2 us -> 8.87 us  [per_device(): lax.psum_scatter(up_acc, ('shard', 'ctx'), scatter_dimension=0, tiled=True)]
    reduce_scatter x1, waiting for transfers between devices: 8.99 us -> 58.2 us  [per_device(): lax.psum_scatter(gate_acc, ('shard', 'ctx'), scatter_dimension=0, tiled=T...]
    all_gather x2, waiting for transfers between devices: 76.7 us -> 38.1 us  [per_device(): upstream_all = lax.all_gather(upstream_b, 'tp', axis=0, tiled=True)]
    all_gather x1, waiting for transfers between devices: 0.03 us -> 23.4 us  [fetch_weights(): lax.all_gather(gate_weight, ('shard', 'ctx'), axis=0, tiled=True)]
    concatenate x0 -> x2, other arithmetic: none -> 19.4 us  [per_device(): jnp.roll(jnp.concatenate(ring[::-1], axis=0), (lax.axis_index('tp') + 1)...]
    reduce_scatter x2, waiting for transfers between devices: 35.6 us -> 52.4 us  [per_device(): lax.psum_scatter(project_pair(gate_back, gate_full, up_back, up_full).ast...]
  transfers between devices with their start and end apart: 34 -> 38, of which waited for: 26 -> 29; matrix products, arithmetic and copies ran while one was open for 27% -> 28% of each run, Pallas kernels for 0% -> 0%
where the time goes in v1:
time: 1630 us
  waiting for transfers between devices  1030 us (63%)
  matrix products  329 us (20%)
  other arithmetic  135 us (8%)
  blocking collectives  83.3 us (5%)
  starting transfers between devices  18.5 us (1%)
  local copies, waits for them, and re-layouts  16.3 us (1%)
    reduce_scatter x2, waiting for transfers between devices, per_device(): lax.psum_scatter(key_buffer.astype(jnp.bfloat16), 'ctx', scatter_dimensio...  206 us
    reduce_scatter x2, waiting for transfers between devices, per_device(): lax.psum_scatter(project_rows(hidden_b, down_full).astype(jnp.bfloat16),...  86 us
    all_gather x2, waiting for transfers between devices, per_device(): first_all = lax.all_gather(first, 'tp', axis=0, tiled=True)  80.4 us
    reduce_scatter x1, waiting for transfers between devices, per_device(): lax.psum_scatter(gate_acc, ('shard', 'ctx'), scatter_dimension=0, tiled=T...  58.2 us
    reduce_scatter x1, waiting for transfers between devices, per_device(): lax.psum_scatter(down_acc, ('shard', 'ctx'), scatter_dimension=1, tiled=T...  57.9 us
    ppermute x6, waiting for transfers between devices, per_device(): lax.ppermute(ring[-1], 'tp', [(dev, (dev + 1) % 4) for dev in range(4)])  56 us
    dot_general x14, matrix products, dot_last(): lax.dot_general(left, right, (((1,), (1,)), ((), ())), preferred_element_...  55.4 us
    dot_general x2, matrix products, update(): jnp.einsum('qkgd,nkd->kgqn', query_b, key_piece, preferred_element_type=j...  53.2 us
  transfers between devices with their start and end apart: 38, of which 29 were waited for; matrix products, arithmetic and copies ran while one was open for 28% of the time, Pallas kernels for 0%

profile of v1, /device:TPU:0, one launch (start us, length us, event | category | flops | bytes accessed | tf_op | source)
XLA Modules:
  0.0 1625.0 jit_solution(14618002352785917022)
XLA Ops:
  25.1 36.1 %all-gather.16.cloned.1.call-done = bf16[1024,1024]{1,0:T(8,128)(2,1)} async-done(((bf16[256,1024]{1,0:T(8,128)(2,1)}), bf16[1024,1024]{1,0:T(8,128)(2,1)}) %all-gather.16.cloned.1.call-update) | async-done | bytes 2097168 | tf_op jit(solution)/shard_map/all_gather | solution.py:204
  63.7 44.2 %all-gather.28.cloned.1.call-done = bf16[1024,1024]{1,0:T(8,128)(2,1)} async-done(((bf16[256,1024]{1,0:T(8,128)(2,1)}), bf16[1024,1024]{1,0:T(8,128)(2,1)}) %all-gather.28.cloned.1.call-update) | async-done | bytes 2097168 | tf_op jit(solution)/shard_map/all_gather | solution.py:204
  164.6 84.7 %conditional.3 = (f32[2,2,1024]{2,1,0:T(2,128)}, f32[2,2,1024]{2,1,0:T(2,128)}, f32[2,2,1024,64]{2,3,1,0:T(8,128)S(1)}, f32[2,2,1024]{2,1,0:T(2,128)S(1)}) conditional(s32[]{:T(128)} %convert_element_type.260, () %tuple.39, (s32[1024]{0:T(1024)S(1)}, bf16[4096,2,64]{0,2,1:T(8,128)(2,1)}, bf16[1024,2,2,64]{0,3,2,1:T(8,128)(2,1)}, ...), branch_computations={%region_13.15_spmd, %region_14.18_spmd} | conditional | flops 4517261312 | bytes 221909024 | solution.py:105
  170.4 27.3 %fusion.16 = (f32[2,2,1024]{2,1,0:T(2,128)S(1)}, f32[2,4096,1024,2]{2,1,3,0:T(8,128)}) fusion(pred[1024,4096]{0,1:T(8,128)(4,1)} %iota_compare_fusion.1, bf16[1024,2,2,64]{0,3,2,1:T(8,128)(2,1)} %get-tuple-element.121, bf16[4096,2,64]{0,2,1:T(8,128)(2,1)} %get-tuple-element.120), kind=kOutput, calls=%fused_computation.19 | convolution fusion | flops 2197811200 | bytes 72892416 | tf_op jit(solution)/shard_map/cond/branch_1_fun/qkgd,nkd->kgqn/dot_general | solution.py:88
  253.2 83.4 %conditional.2 = (f32[2,2,1024]{2,1,0:T(2,128)}, f32[2,2,1024]{2,1,0:T(2,128)}, f32[2,2,1024,64]{2,3,1,0:T(8,128)S(1)}, f32[2,2,1024]{2,1,0:T(2,128)S(1)}) conditional(s32[]{:T(128)} %convert_element_type.260, () %tuple.37, (s32[1024]{0:T(1024)S(1)}, bf16[4096,2,64]{0,2,1:T(8,128)(2,1)}, bf16[1024,2,2,64]{0,3,2,1:T(8,128)(2,1)S(1)}, ...), branch_computations={%region_3.0_spmd, %region_4.7_spmd} | conditional | flops 4517261312 | bytes 230297696 | solution.py:105
  343.9 38.7 %reduce-scatter.20.cloned.1.call-done = bf16[256,1024]{1,0:T(8,128)(2,1)} async-done(((bf16[1024,1024]{1,0:T(8,128)(2,1)}), bf16[256,1024]{1,0:T(8,128)(2,1)}) %reduce-scatter.20.cloned.1.call-update) | async-done | bytes 524304 | tf_op jit(solution)/shard_map/reduce_scatter | solution.py:231
  464.2 29.4 %all-gather.26.cloned.1.call-done = bf16[1152,1024]{1,0:T(8,128)(2,1)} async-done(((bf16[1152,128]{1,0:T(8,128)(2,1)}), bf16[1152,1024]{1,0:T(8,128)(2,1)}) %all-gather.26.cloned.1.call-update) | async-done | bytes 2359312 | tf_op jit(solution)/shard_map/all_gather | solution.py:68
  574.1 29.3 %all-gather.38.cloned.1.call-done = bf16[1,1024,1024]{2,1,0:T(8,128)(2,1)} async-done(((bf16[1,256,1024]{2,1,0:T(8,128)(2,1)}), bf16[1,1024,1024]{2,1,0:T(8,128)(2,1)}) %all-gather.38.cloned.1.call-update) | async-done | bytes 2097168 | tf_op jit(solution)/shard_map/all_gather | solution.py:270
  648.2 46.0 %reduce-scatter.28.cloned.1.call-done = bf16[256,1024]{1,0:T(8,128)(2,1)} async-done(((bf16[1024,1024]{1,0:T(8,128)(2,1)}), bf16[256,1024]{1,0:T(8,128)(2,1)}) %reduce-scatter.28.cloned.1.call-update) | async-done | bytes 524304 | tf_op jit(solution)/shard_map/reduce_scatter | solution.py:279
  697.0 42.6 %reduce-scatter.26.cloned.1.call-done = bf16[256,1024]{1,0:T(8,128)(2,1)} async-done(((bf16[1024,1024]{1,0:T(8,128)(2,1)}), bf16[256,1024]{1,0:T(8,128)(2,1)}) %reduce-scatter.26.cloned.1.call-update) | async-done | bytes 524304 | tf_op jit(solution)/shard_map/reduce_scatter | solution.py:252
  744.9 43.8 %all-gather.36.cloned.1.call-done = bf16[1024,1024]{1,0:T(8,128)(2,1)} async-done(((bf16[256,1024]{1,0:T(8,128)(2,1)}), bf16[1024,1024]{1,0:T(8,128)(2,1)}) %all-gather.36.cloned.1.call-update) | async-done | bytes 2097168 | tf_op jit(solution)/shard_map/all_gather | solution.py:289
  793.7 34.4 %while.31 = (s32[]{:T(128)}, f32[1024,2,2,64]{0,3,2,1:T(8,128)S(1)}, bf16[4096,2,64]{0,2,1:T(8,128)(2,1)}, bf16[4096,2,64]{0,2,1:T(8,128)(2,1)}, s32[]{:T(128)},...) while((s32[]{:T(128)}, ...), condition=%wide.region_33.35_spmd.clone, body=%wide.region_32.34_spmd.clone.sunk | while | flops 2728003584 | bytes 93126936 | solution.py:155
  841.2 33.8 %while.30 = (s32[]{:T(128)}, f32[1024,2,2,64]{0,3,2,1:T(8,128)S(1)}, bf16[4096,2,64]{0,2,1:T(8,128)(2,1)}, bf16[4096,2,64]{0,2,1:T(8,128)(2,1)}, s32[]{:T(128)},...) while((s32[]{:T(128)}, ...), condition=%wide.region_23.25_spmd.clone, body=%wide.region_22.24_spmd.clone.sunk | while | flops 2728003584 | bytes 99418456 | solution.py:155
  888.2 66.5 %reduce-scatter.38.cloned.1.call-done = bf16[1024,2,64]{0,2,1:T(8,128)(2,1)} async-done(((bf16[4096,2,64]{0,2,1:T(8,128)(2,1)}), bf16[1024,2,64]{0,2,1:T(8,128)(2,1)}) %reduce-scatter.38.cloned.1.call-update) | async-done | bytes 262160 | tf_op jit(solution)/shard_map/reduce_scatter | solution.py:304
  955.8 139.6 %reduce-scatter.30.cloned.1.call-done = bf16[1024,2,64]{0,2,1:T(8,128)(2,1)} async-done(((bf16[4096,2,64]{0,2,1:T(8,128)(2,1)}), bf16[1024,2,64]{0,2,1:T(8,128)(2,1)}) %reduce-scatter.30.cloned.1.call-update) | async-done | bytes 262160 | tf_op jit(solution)/shard_map/reduce_scatter | solution.py:304
  1210.8 31.9 %reduce-scatter.34.cloned.1.call-done = bf16[256,1024]{1,0:T(8,128)(2,1)} async-done(((bf16[1024,1024]{1,0:T(8,128)(2,1)}), bf16[256,1024]{1,0:T(8,128)(2,1)}) %reduce-scatter.34.cloned.1.call-update) | async-done | bytes 524304 | tf_op jit(solution)/shard_map/reduce_scatter | solution.py:323
  1244.9 43.4 %reduce-scatter.22.cloned.1.call-done = bf16[256,1024]{1,0:T(8,128)(2,1)} async-done(((bf16[1024,1024]{1,0:T(8,128)(2,1)}), bf16[256,1024]{1,0:T(8,128)(2,1)}) %reduce-scatter.22.cloned.1.call-update) | async-done | bytes 524304 | tf_op jit(solution)/shard_map/reduce_scatter | solution.py:252
  1291.6 39.9 %all-reduce.8 = (f32[1024]{0:T(1024)}, f32[1024]{0:T(1024)}, f32[64]{0:T(128)}, f32[64]{0:T(128)}) all-reduce(f32[1024]{0:T(1024)S(1)} %add.382, f32[1024]{0:T(1024)S(1)} %add.383, f32[64]{0:T(128)S(1)} %add.384, f32[64]{0:T(128)S(1)} %add.385), channel_id=1, replica_groups=mesh['shard'=2,'ctx'=4,'tp'=4] {'shard','ctx','tp'}, use_global_device_ids=true, to_apply=%region_49.51 | all-reduce | flops 2176 | bytes 17408 | tf_op jit(solution)/shard_map/psum | solution.py:344
  1346.1 58.2 %reduce-scatter.52.cloned.1.call-done = f32[128,1152]{1,0:T(8,128)} async-done(((f32[1024,1152]{1,0:T(8,128)}), f32[128,1152]{1,0:T(8,128)}) %reduce-scatter.52.cloned.1.call-update) | async-done | bytes 589840 | tf_op jit(solution)/shard_map/reduce_scatter | solution.py:340
  1404.3 57.9 %reduce-scatter.56.cloned.1.call-done = f32[1152,128]{1,0:T(8,128)} async-done(((f32[1152,1024]{1,0:T(8,128)}), f32[1152,128]{1,0:T(8,128)}) %reduce-scatter.56.cloned.1.call-update) | async-done | bytes 589840 | tf_op jit(solution)/shard_map/reduce_scatter | solution.py:342
  1462.2 40.1 %reduce-scatter.50.cloned.1.call-done = f32[256,128]{1,0:T(8,128)} async-done(((f32[256,1024]{1,0:T(8,128)}), f32[256,128]{1,0:T(8,128)}) %reduce-scatter.50.cloned.1.call-update) | async-done | bytes 131088 | tf_op jit(solution)/shard_map/reduce_scatter | solution.py:339
  1502.3 40.0 %reduce-scatter.44.cloned.1.call-done = f32[128,256]{1,0:T(8,128)} async-done(((f32[1024,256]{1,0:T(8,128)}), f32[128,256]{1,0:T(8,128)}) %reduce-scatter.44.cloned.1.call-update) | async-done | bytes 131088 | tf_op jit(solution)/shard_map/reduce_scatter | solution.py:336
  1542.3 38.1 %reduce-scatter.48.cloned.1.call-done = f32[128,128]{1,0:T(8,128)} async-done(((f32[1024,128]{1,0:T(8,128)}), f32[128,128]{1,0:T(8,128)}) %reduce-scatter.48.cloned.1.call-update) | async-done | bytes 65552 | tf_op jit(solution)/shard_map/reduce_scatter | solution.py:338
  1580.4 37.8 %reduce-scatter.46.cloned.1.call-done = f32[128,128]{1,0:T(8,128)} async-done(((f32[1024,128]{1,0:T(8,128)}), f32[128,128]{1,0:T(8,128)}) %reduce-scatter.46.cloned.1.call-update) | async-done | bytes 65552 | tf_op jit(solution)/shard_map/reduce_scatter | solution.py:337
  (499 shorter events, 677.5 us)
Async XLA Ops:
  13.2 151.4 %all-gather.30.cloned.1.call-start = ((), (), s32[]{:S(2)}) async-start(), calls=%async_computation.28 | async-start | bytes 1310720 | tf_op jit(solution)/shard_map/all_gather | solution.py:82
  125.3 127.8 %all-gather.18.cloned.1.call-start = ((), (), s32[]{:S(2)}) async-start(), calls=%async_computation.20 | async-start | bytes 1310720 | tf_op jit(solution)/shard_map/all_gather | solution.py:82
  155.7 188.1 %reduce-scatter.24.cloned.1.call-start = ((), (), s32[]{:S(2)}) async-start(), calls=%async_computation.30 | async-start | bytes 2621440 | tf_op jit(solution)/shard_map/reduce_scatter | solution.py:231
  252.9 129.7 %reduce-scatter.20.cloned.1.call-start = ((), (), s32[]{:S(2)}) async-start(), calls=%async_computation.22 | async-start | bytes 2621440 | tf_op jit(solution)/shard_map/reduce_scatter | solution.py:231
  339.6 124.6 %all-gather.40.cloned.1.call-start = ((), (), s32[]{:S(2)}) async-start(), calls=%async_computation.50 | async-start | bytes 2621440 | tf_op jit(solution)/shard_map/all_gather | solution.py:270
  341.9 151.7 %all-gather.26.cloned.1.call-start = ((), (), s32[]{:S(2)}) async-start(), calls=%async_computation.25 | async-start | bytes 2654208 | tf_op jit(solution)/shard_map/all_gather | solution.py:68
  342.5 182.0 %all-gather.24.cloned.1.call-start = ((), (), s32[]{:S(2)}) async-start(), calls=%async_computation.24 | async-start | bytes 2654208 | tf_op jit(solution)/shard_map/all_gather | solution.py:67
  343.2 212.1 %all-gather.22.cloned.1.call-start = ((), (), s32[]{:S(2)}) async-start(), calls=%async_computation.23 | async-start | bytes 2654208 | tf_op jit(solution)/shard_map/all_gather | solution.py:66
  343.8 259.6 %all-gather.38.cloned.1.call-start = ((), (), s32[]{:S(2)}) async-start(), calls=%async_computation.49 | async-start | bytes 2621440 | tf_op jit(solution)/shard_map/all_gather | solution.py:270
  411.0 237.2 %reduce-scatter.36.cloned.1.call-start = ((), (), s32[]{:S(2)}) async-start(), calls=%async_computation.37 | async-start | bytes 2621440 | tf_op jit(solution)/shard_map/reduce_scatter | solution.py:279
  641.7 146.9 %all-gather.36.cloned.1.call-start = ((), (), s32[]{:S(2)}) async-start(), calls=%async_computation.38 | async-start | bytes 2621440 | tf_op jit(solution)/shard_map/all_gather | solution.py:289
  744.8 209.9 %reduce-scatter.38.cloned.1.call-start = ((), (), s32[]{:S(2)}) async-start(), calls=%async_computation.39 | async-start | bytes 1310720 | tf_op jit(solution)/shard_map/reduce_scatter | solution.py:304
  828.1 267.3 %reduce-scatter.30.cloned.1.call-start = ((), (), s32[]{:S(2)}) async-start(), calls=%async_computation.34 | async-start | bytes 1310720 | tf_op jit(solution)/shard_map/reduce_scatter | solution.py:304
  875.0 248.0 %reduce-scatter.40.cloned.1.call-start = ((), (), s32[]{:S(2)}) async-start(), calls=%async_computation.40 | async-start | bytes 1310720 | tf_op jit(solution)/shard_map/reduce_scatter | solution.py:307
  878.5 272.0 %reduce-scatter.32.cloned.1.call-start = ((), (), s32[]{:S(2)}) async-start(), calls=%async_computation.35 | async-start | bytes 1310720 | tf_op jit(solution)/shard_map/reduce_scatter | solution.py:307
  888.1 322.6 %reduce-scatter.42.cloned.1.call-start = ((), (), s32[]{:S(2)}) async-start(), calls=%async_computation.41 | async-start | bytes 2621440 | tf_op jit(solution)/shard_map/reduce_scatter | solution.py:323
  1156.1 132.2 %reduce-scatter.22.cloned.1.call-start = ((), (), s32[]{:S(2)}) async-start(), calls=%async_computation.26 | async-start | bytes 2621440 | tf_op jit(solution)/shard_map/reduce_scatter | solution.py:252
  1162.8 183.3 %reduce-scatter.54.cloned.1.call-start = ((), (), s32[]{:S(2)}) async-start(), calls=%async_computation.47 | async-start | bytes 5308416 | tf_op jit(solution)/shard_map/reduce_scatter | solution.py:341
  1173.5 230.7 %reduce-scatter.52.cloned.1.call-start = ((), (), s32[]{:S(2)}) async-start(), calls=%async_computation.46 | async-start | bytes 5308416 | tf_op jit(solution)/shard_map/reduce_scatter | solution.py:340
  1183.9 278.3 %reduce-scatter.56.cloned.1.call-start = ((), (), s32[]{:S(2)}) async-start(), calls=%async_computation.48 | async-start | bytes 5308416 | tf_op jit(solution)/shard_map/reduce_scatter | solution.py:342
  1193.5 308.8 %reduce-scatter.50.cloned.1.call-start = ((), (), s32[]{:S(2)}) async-start(), calls=%async_computation.45 | async-start | bytes 1179648 | tf_op jit(solution)/shard_map/reduce_scatter | solution.py:339
  1200.2 342.1 %reduce-scatter.44.cloned.1.call-start = ((), (), s32[]{:S(2)}) async-start(), calls=%async_computation.42 | async-start | bytes 1179648 | tf_op jit(solution)/shard_map/reduce_scatter | solution.py:336
  1203.8 376.7 %reduce-scatter.48.cloned.1.call-start = ((), (), s32[]{:S(2)}) async-start(), calls=%async_computation.44 | async-start | bytes 589824 | tf_op jit(solution)/shard_map/reduce_scatter | solution.py:338
  1207.4 410.8 %reduce-scatter.46.cloned.1.call-start = ((), (), s32[]{:S(2)}) async-start(), calls=%async_computation.43 | async-start | bytes 589824 | tf_op jit(solution)/shard_map/reduce_scatter | solution.py:337
  (146 other events, 6892.7 us)
Sparse Core Ops, SparseCore 0:
  12.5 48.6 all-gather.15
  63.3 44.5 all-gather.27
  253.0 42.7 reduce-scatter.23
  339.7 42.8 reduce-scatter.19
  384.7 79.4 all-gather.39
  495.5 29.0 all-gather.23
  557.5 45.9 all-gather.37
  605.6 42.5 reduce-scatter.35
  651.0 43.1 reduce-scatter.27
  696.4 43.1 reduce-scatter.25
  743.4 45.2 all-gather.35
  790.7 44.6 all-gather.33
  838.1 116.5 reduce-scatter.37
  957.6 137.7 reduce-scatter.29
  1152.9 43.8 reduce-scatter.41
  1199.5 43.1 reduce-scatter.33
  1245.1 43.1 reduce-scatter.21
  1292.2 53.8 reduce-scatter.53
  1350.3 53.8 reduce-scatter.51
  1408.3 53.8 reduce-scatter.55
  1466.3 35.9 reduce-scatter.49
  1506.3 36.0 reduce-scatter.43
  1546.3 34.1 reduce-scatter.47
  1584.1 34.1 reduce-scatter.45
  (8 shorter events, 173.6 us)
